TPU v7x, 32 devices: a whole 2x2x4 slice. The times are simulated.
32 devices in a mesh: row: 2 (over x), col: 16 (over z, y, core).
Axes of the slice: x: 2, y: 2, z: 4, core: 2. Of those that a mesh axis runs over, the one named last changes fastest.
Arguments:
- features: bfloat16 [64, 768, 256], P('row', 'col'), may hold values from -6 to 6
- conv_one: bfloat16 [3, 3, 256, 256], replicated, may hold values from -0.125 to 0.125
- bias_one: float32 [256], replicated, may hold values from -3 to 3
- conv_two: bfloat16 [3, 3, 256, 512], replicated, may hold values from -0.125 to 0.125
- bias_two: float32 [512], replicated, may hold values from -3 to 3
- conv_three: bfloat16 [16, 3, 3, 32, 32], P('col'), may hold values from -0.375 to 0.375
- bias_three: float32 [512], P('col'), may hold values from -3 to 3
Outputs:
- encoded: bfloat16 [32, 512, 384], P('row', 'col')
All inputs are finite; a program needn't handle non-finite values.
Results may differ from a plain program's by a relative error of at most 0.0051.
Values may be sent and summed in bfloat16 or wider, within the bound.
A program may use at most 64 MiB of HBM per device.

v0:
```python
import jax
import jax.numpy as jnp
from jax import lax
from jax.sharding import PartitionSpec as P


def padded_2(block, sides, width):
    for axis, dim in sides:
        count = lax.axis_size(axis)
        forward = [(i, i + 1) for i in range(count - 1)]
        backward = [(target, source) for source, target in forward]
        low = lax.ppermute(
            lax.slice_in_dim(block, block.shape[dim] - width, None, axis=dim), axis, forward
        )
        high = lax.ppermute(lax.slice_in_dim(block, 0, width, axis=dim), axis, backward)
        block = jnp.concatenate([low, block, high], axis=dim)
    return block


def passed_along(block, axis, distance):
    devices = range(lax.axis_size(axis))
    route = [(i - distance, i) for i in devices if i - distance in devices]
    return lax.ppermute(block, axis, route)


def conv_taps(padded, weight, out_rows, out_cols, stride):
    summed = None
    for tap_row in range(3):
        for tap_col in range(3):
            window = lax.slice(
                padded,
                (tap_row, tap_col, 0),
                (
                    tap_row + stride * (out_rows - 1) + 1,
                    tap_col + stride * (out_cols - 1) + 1,
                    padded.shape[2],
                ),
                (stride, stride, 1),
            )
            product = jnp.dot(
                window.reshape(out_rows * out_cols, padded.shape[2]),
                weight[tap_row, tap_col],
                preferred_element_type=jnp.float32,
            )
            summed = product if summed is None else summed + product
    return summed.reshape(out_rows, out_cols, weight.shape[3])


def on_device(features, conv_one, bias_one, conv_two, bias_two, conv_three, bias_three):
    tile_rows = features.shape[0]
    tile_cols = features.shape[1]
    padded = padded_2(features, (("row", 0), ("col", 1)), 1)
    summed = conv_taps(padded, conv_one, tile_rows, tile_cols, 1)
    layer_one = jax.nn.relu(summed + bias_one).astype(jnp.bfloat16)
    upper_row = passed_along(layer_one[tile_rows - 1 :], "row", 1)
    extended = jnp.concatenate([upper_row, layer_one], 0)
    left_column = passed_along(extended[:, tile_cols - 1 :], "col", 1)
    extended = jnp.concatenate([left_column, extended], 1)
    summed = conv_taps(extended, conv_two, tile_rows // 2, tile_cols // 2, 2)
    layer_two = jax.nn.relu(summed + bias_two).astype(jnp.bfloat16)
    grouped = lax.all_to_all(layer_two, "col", split_axis=2, concat_axis=1, tiled=True)
    grouped = padded_2(grouped, (("row", 0),), 1)
    grouped = jnp.pad(grouped, ((0, 0), (1, 1), (0, 0)))
    local_groups = conv_three.shape[0]
    group_width = conv_three.shape[3]
    out_rows = layer_two.shape[0]
    full_cols = grouped.shape[1] - 2
    summed = None
    for tap_row in range(3):
        for tap_col in range(3):
            window = grouped[tap_row : tap_row + out_rows, tap_col : tap_col + full_cols].reshape(
                out_rows, full_cols, local_groups, group_width
            )
            product = jnp.einsum(
                "rwgi,gio->rgow",
                window,
                conv_three[:, tap_row, tap_col],
                preferred_element_type=jnp.float32,
            )
            summed = product if summed is None else summed + product
    result = (
        summed.reshape(out_rows, local_groups * group_width, full_cols) + bias_three[None, :, None]
    )
    return result.astype(jnp.bfloat16)


def solution(mesh):
    in_specs = (
        P("row", "col", None),
        P(),
        P(),
        P(),
        P(),
        P("col", None, None, None, None),
        P("col"),
    )
    out_specs = P("row", "col", None)
    return jax.shard_map(
        on_device, mesh=mesh, in_specs=in_specs, out_specs=out_specs, check_vma=False
    )
```

profile of v0, /device:TPU:0, one launch (start us, length us, event | category | flops | bytes accessed | tf_op | source)
XLA Modules:
  0.0 93.5 jit_solution(4920264722464064641)
XLA Ops:
  0.8 4.9 %collective-permute-start = (bf16[1,48,256]{2,1,0:T(8,128)(2,1)S(1)}, bf16[1,48,256]{2,1,0:T(8,128)(2,1)S(1)}, u32[]{:S(2)}, u32[]{:S(2)}) collective-permute-start(bf16[1,48,256]{2,1,0:T(8,128)(2,1)S(1)} %get-tuple-element.22), channel_id=1, source_target_pairs={{0,16},{1,17},{2,18},{3,19},{4,20},{5,21},{6,22},{7,23},{8,24},{9,... | collective-permute-start | bytes 73736 | tf_op jit(solution)/shard_map/ppermute | solution.py:12
  5.6 1.3 %collective-permute-start.1 = (bf16[1,48,256]{2,1,0:T(8,128)(2,1)S(1)}, bf16[1,48,256]{2,1,0:T(8,128)(2,1)S(1)}, u32[]{:S(2)}, u32[]{:S(2)}) collective-permute-start(bf16[1,48,256]{2,1,0:T(8,128)(2,1)S(1)} %get-tuple-element.21), channel_id=1, source_target_pairs={{16,0},{17,1},{18,2},{19,3},{20,4},{21,5},{22,6},{23,7},{24,8},{25... | collective-permute-start | bytes 73736 | tf_op jit(solution)/shard_map/ppermute | solution.py:15
  7.1 4.2 %collective-permute-done.1 = bf16[1,48,256]{2,1,0:T(8,128)(2,1)S(1)} collective-permute-done((bf16[1,48,256]{2,1,0:T(8,128)(2,1)S(1)}, bf16[1,48,256]{2,1,0:T(8,128)(2,1)S(1)}, u32[]{:S(2)}, u32[]{:S(2)}) %collective-permute-start.1) | collective-permute-done | bytes 24608 | tf_op jit(solution)/shard_map/ppermute | solution.py:15
  11.3 2.2 %pad_maximum_fusion.4 = (bf16[32,48,256]{2,1,0:T(8,128)(2,1)S(1)}, bf16[32,48,256]{2,1,0:T(8,128)(2,1)S(1)}, bf16[34,48,256]{2,1,0:T(8,128)(2,1)S(1)}) fusion(bf16[32,48,256]{2,1,0:T(8,128)(2,1)} %param.7, bf16[1,48,256]{2,1,0:T(8,128)(2,1)S(1)} %collective-permute-done, bf16[1,48,256]{2,1,0:T(8,128)(2,1)S(1)} %collective-permute-done.1, ...), kind=kLoop, calls=%fused_computation.49 | loop fusion | flops 3145728 | bytes 3194880 | tf_op jit(solution)/shard_map/concatenate | solution.py:16
  13.6 1.3 %collective-permute-start.2 = (bf16[34,1,256]{2,1,0:T(2,128)(2,1)S(1)}, bf16[34,1,256]{2,1,0:T(2,128)(2,1)S(1)}, u32[]{:S(2)}, u32[]{:S(2)}) collective-permute-start(bf16[34,1,256]{2,1,0:T(2,128)(2,1)S(1)} %get-tuple-element.16), channel_id=1, source_target_pairs={{0,1},{1,2},{2,3},{3,4},{4,5},{5,6},{6,7},{7,8},{8,9},{9,10},{10,1... | collective-permute-start | bytes 52232 | tf_op jit(solution)/shard_map/ppermute | solution.py:12
  14.9 1.3 %collective-permute-start.3 = (bf16[34,1,256]{2,1,0:T(2,128)(2,1)S(1)}, bf16[34,1,256]{2,1,0:T(2,128)(2,1)S(1)}, u32[]{:S(2)}, u32[]{:S(2)}) collective-permute-start(bf16[34,1,256]{2,1,0:T(2,128)(2,1)S(1)} %get-tuple-element.17), channel_id=1, source_target_pairs={{1,0},{2,1},{3,2},{4,3},{5,4},{6,5},{7,6},{8,7},{9,8},{10,9},{11,1... | collective-permute-start | bytes 52232 | tf_op jit(solution)/shard_map/ppermute | solution.py:15
  17.0 2.8 %collective-permute-done.3 = bf16[34,1,256]{2,1,0:T(2,128)(2,1)S(1)} collective-permute-done((bf16[34,1,256]{2,1,0:T(2,128)(2,1)S(1)}, bf16[34,1,256]{2,1,0:T(2,128)(2,1)S(1)}, u32[]{:S(2)}, u32[]{:S(2)}) %collective-permute-start.3) | collective-permute-done | bytes 17440 | tf_op jit(solution)/shard_map/ppermute | solution.py:15
  19.8 2.9 %pad_maximum_fusion.3 = (bf16[32,48,256]{2,1,0:T(8,128)(2,1)S(1)}, bf16[32,48,256]{2,1,0:T(8,128)(2,1)S(1)}, bf16[32,48,256]{2,1,0:T(8,128)(2,1)S(1)}, bf16[32,4...) fusion(bf16[34,48,256]{2,1,0:T(8,128)(2,1)S(1)} %constant_dynamic-update-slice_fusion,, ...), kind=kLoop, calls=%fused_computation.48 | loop fusion | flops 9437184 | bytes 5588992 | tf_op jit(solution)/shard_map/concatenate | solution.py:16
  26.6 1.6 %collective-permute-start.4 = (bf16[1,48,256]{2,1,0:T(8,128)(2,1)S(1)}, bf16[1,48,256]{2,1,0:T(8,128)(2,1)S(1)}, u32[]{:S(2)}, u32[]{:S(2)}) collective-permute-start(bf16[1,48,256]{2,1,0:T(8,128)(2,1)S(1)} %slice.272), channel_id=1, source_target_pairs={{0,16},{1,17},{2,18},{3,19},{4,20},{5,21},{6,22},{7,23},{8,24},{9,... | collective-permute-start | bytes 73736 | tf_op jit(solution)/shard_map/ppermute | solution.py:23
  31.1 4.3 %collective-permute-start.5 = (bf16[33,1,256]{2,1,0:T(2,128)(2,1)S(1)}, bf16[33,1,256]{2,1,0:T(2,128)(2,1)S(1)}, u32[]{:S(2)}, u32[]{:S(2)}) collective-permute-start(bf16[33,1,256]{2,1,0:T(2,128)(2,1)S(1)} %fusion.66), channel_id=1, source_target_pairs={{0,1},{1,2},{2,3},{3,4},{4,5},{5,6},{6,7},{7,8},{8,9},{9,10},{10,1... | collective-permute-start | bytes 50696 | tf_op jit(solution)/shard_map/ppermute | solution.py:23
  36.0 1.2 %fusion.33 = f32[384,512]{1,0:T(8,128)S(1)} fusion(bf16[384,256]{1,0:T(8,128)(2,1)S(1)} %bitcast.192, bf16[3,3,256,512]{3,2,1,0:T(8,128)(2,1)} %param.10), kind=kOutput, calls=%fused_computation.76 | convolution fusion | flops 100663296 | bytes 1245184 | tf_op jit(solution)/shard_map/dot_general | solution.py:40
  37.2 5.0 %slice.227 = bf16[16,24,256]{2,1,0:T(8,128)(2,1)} slice(bf16[33,48,256]{2,1,0:T(8,128)(2,1)S(1)} %pad_maximum_fusion), slice={[0:31:2], [1:48:2], [0:256:1]} | slice | bytes 393216 | tf_op jit(solution)/shard_map/slice | solution.py:30
  44.5 1.4 %convolution_add_fusion.20 = f32[384,512]{1,0:T(8,128)S(1)} fusion(f32[384,512]{1,0:T(8,128)S(1)} %fusion.33, bf16[384,256]{1,0:T(8,128)(2,1)S(1)} %bitcast.200, bf16[3,3,256,512]{3,2,1,0:T(8,128)(2,1)} %param.10), kind=kOutput, calls=%fused_computation.32 | convolution fusion | flops 100859904 | bytes 2031616 | tf_op jit(solution)/shard_map/dot_general | solution.py:40
  45.9 1.2 %convolution_add_fusion.19 = f32[384,512]{1,0:T(8,128)S(1)} fusion(f32[384,512]{1,0:T(8,128)S(1)} %convolution_add_fusion.20, bf16[384,256]{1,0:T(8,128)(2,1)S(1)} %bitcast.197, bf16[3,3,256,512]{3,2,1,0:T(8,128)(2,1)} %param.10), kind=kOutput, calls=%fused_computation.31 | convolution fusion | flops 100859904 | bytes 2031616 | tf_op jit(solution)/shard_map/dot_general | solution.py:40
  48.9 2.0 %copy.53 = bf16[16,24,512]{1,0,2:T(8,128)(2,1)S(1)} copy(bf16[16,24,512]{2,1,0:T(8,128)(2,1)S(1)} %maximum_convert_fusion.1) | data formatting | bytes 786432 | tf_op jit(solution)/shard_map/convert_element_type | solution.py:60
  50.9 2.7 %reshape.188 = bf16[16,2,6144]{2,1,0:T(2,128)(2,1)S(1)} reshape(bf16[512,16,24]{2,1,0:T(8,128)(2,1)S(1)} %bitcast.179) | data formatting | bytes 786432
  53.6 17.8 %all_to_all.18 = bf16[16,2,6144]{2,1,0:T(2,128)(2,1)S(1)} all-to-all(bf16[16,2,6144]{2,1,0:T(2,128)(2,1)S(1)} %reshape.188), channel_id=1, replica_groups=mesh['row'=2,'col'=16] {'col'}, dimensions={0} | all-to-all | bytes 786432 | tf_op jit(solution)/shard_map/all_to_all | solution.py:61
  71.5 3.0 %reshape.189 = bf16[512,16,24]{2,1,0:T(8,128)(2,1)S(1)} reshape(bf16[16,2,6144]{2,1,0:T(2,128)(2,1)S(1)} %all_to_all.18) | data formatting | bytes 786432
  74.4 3.1 %copy.67 = bf16[16,24,16,32]{3,2,1,0:T(8,128)(2,1)} copy(bf16[16,24,16,32]{1,0,3,2:T(8,128)(2,1)S(1)} %bitcast.177) | data formatting | bytes 786432 | tf_op jit(solution)/shard_map/all_to_all | solution.py:61
  78.8 2.8 %collective-permute-start.6 = (bf16[1,384,32]{1,2,0:T(8,128)(2,1)S(1)}, bf16[1,384,32]{1,2,0:T(8,128)(2,1)S(1)}, u32[]{:S(2)}, u32[]{:S(2)}) collective-permute-start(bf16[1,384,32]{1,2,0:T(8,128)(2,1)S(1)} %slice.242), channel_id=1, source_target_pairs={{0,16},{1,17},{2,18},{3,19},{4,20},{5,21},{6,22},{7,23},{8,24},{9,... | collective-permute-start | bytes 73736 | tf_op jit(solution)/shard_map/ppermute | solution.py:12
  82.0 1.5 %collective-permute-start.7 = (bf16[1,384,32]{1,2,0:T(8,128)(2,1)S(1)}, bf16[1,384,32]{1,2,0:T(8,128)(2,1)S(1)}, u32[]{:S(2)}, u32[]{:S(2)}) collective-permute-start(bf16[1,384,32]{1,2,0:T(8,128)(2,1)S(1)} %slice.244), channel_id=1, source_target_pairs={{16,0},{17,1},{18,2},{19,3},{20,4},{21,5},{22,6},{23,7},{24,8},{25... | collective-permute-start | bytes 73736 | tf_op jit(solution)/shard_map/ppermute | solution.py:15
  83.5 2.7 %copy.56 = bf16[16,16,24,32]{2,1,3,0:T(8,128)(2,1)} copy(bf16[16,16,24,32]{2,0,3,1:T(8,128)(2,1)S(1)} %bitcast.178) | data formatting | bytes 786432 | tf_op jit(solution)/shard_map/all_to_all | solution.py:61
  86.2 3.4 %all_to_all.16 = bf16[16,384,32]{1,2,0:T(8,128)(2,1)S(1)} reshape(bf16[16,16,24,32]{2,1,3,0:T(8,128)(2,1)} %copy.56) | data formatting | bytes 786432 | tf_op jit(solution)/shard_map/all_to_all | solution.py:61
  92.5 1.0 %fusion.5 = bf16[16,32,384]{2,1,0:T(8,128)(2,1)} fusion(f32[16,384,32]{1,2,0:T(8,128)S(1)} %fusion.16, f32[16,384,32]{1,2,0:T(8,128)S(1)} %convolution_add_fusion.7, bf16[1,384,32]{1,2,0:T(8,128)(2,1)S(1)} %collective-permute-done.7, bf16[16,384,32]{1,2,0:T(8,128)(2,1)S(1)} %all_to_all.16, f32[32]{0:T(128)S(1)} %copy-done.7, ...), kind=kOutput, calls=%fused_computation.33 | convolution fusion | flops 14155776 | bytes 2392576 | tf_op jit(solution)/shard_map/rwgi,gio->rgow/dot_general | solution.py:74
  (69 shorter events, 17.4 us)
Async XLA Ops:
  0.8 6.4 %collective-permute-start = (bf16[1,48,256]{2,1,0:T(8,128)(2,1)S(1)}, bf16[1,48,256]{2,1,0:T(8,128)(2,1)S(1)}, u32[]{:S(2)}, u32[]{:S(2)}) collective-permute-start(bf16[1,48,256]{2,1,0:T(8,128)(2,1)S(1)} %get-tuple-element.22), channel_id=1, source_target_pairs={{0,16},{1,17},{2,18},{3,19},{4,20},{5,21},{6,22},{7,23},{8,24},{9,... | collective-permute-start | bytes 73736 | tf_op jit(solution)/shard_map/ppermute | solution.py:12
  5.6 5.7 %collective-permute-start.1 = (bf16[1,48,256]{2,1,0:T(8,128)(2,1)S(1)}, bf16[1,48,256]{2,1,0:T(8,128)(2,1)S(1)}, u32[]{:S(2)}, u32[]{:S(2)}) collective-permute-start(bf16[1,48,256]{2,1,0:T(8,128)(2,1)S(1)} %get-tuple-element.21), channel_id=1, source_target_pairs={{16,0},{17,1},{18,2},{19,3},{20,4},{21,5},{22,6},{23,7},{24,8},{25... | collective-permute-start | bytes 73736 | tf_op jit(solution)/shard_map/ppermute | solution.py:15
  7.1 9.1 %copy-start.2 = (bf16[3,3,256,256]{3,2,1,0:T(8,128)(2,1)S(1)}, bf16[3,3,256,256]{3,2,1,0:T(8,128)(2,1)}, u32[]{:S(2)}) copy-start(bf16[3,3,256,256]{3,2,1,0:T(8,128)(2,1)} %param.8) | copy-start | bytes 3538948
  13.6 3.3 %collective-permute-start.2 = (bf16[34,1,256]{2,1,0:T(2,128)(2,1)S(1)}, bf16[34,1,256]{2,1,0:T(2,128)(2,1)S(1)}, u32[]{:S(2)}, u32[]{:S(2)}) collective-permute-start(bf16[34,1,256]{2,1,0:T(2,128)(2,1)S(1)} %get-tuple-element.16), channel_id=1, source_target_pairs={{0,1},{1,2},{2,3},{3,4},{4,5},{5,6},{6,7},{7,8},{8,9},{9,10},{10,1... | collective-permute-start | bytes 52232 | tf_op jit(solution)/shard_map/ppermute | solution.py:12
  14.9 4.9 %collective-permute-start.3 = (bf16[34,1,256]{2,1,0:T(2,128)(2,1)S(1)}, bf16[34,1,256]{2,1,0:T(2,128)(2,1)S(1)}, u32[]{:S(2)}, u32[]{:S(2)}) collective-permute-start(bf16[34,1,256]{2,1,0:T(2,128)(2,1)S(1)} %get-tuple-element.17), channel_id=1, source_target_pairs={{1,0},{2,1},{3,2},{4,3},{5,4},{6,5},{7,6},{8,7},{9,8},{10,9},{11,1... | collective-permute-start | bytes 52232 | tf_op jit(solution)/shard_map/ppermute | solution.py:15
  23.8 1.1 %copy-start = (bf16[32,48,256]{2,1,0:T(8,128)(2,1)S(1)}, bf16[32,48,256]{2,1,0:T(8,128)(2,1)}, u32[]{:S(2)}) copy-start(bf16[32,48,256]{2,1,0:T(8,128)(2,1)} %param.7) | copy-start | bytes 2359300
  25.7 0.7 copy-start.6
  26.6 4.4 %collective-permute-start.4 = (bf16[1,48,256]{2,1,0:T(8,128)(2,1)S(1)}, bf16[1,48,256]{2,1,0:T(8,128)(2,1)S(1)}, u32[]{:S(2)}, u32[]{:S(2)}) collective-permute-start(bf16[1,48,256]{2,1,0:T(8,128)(2,1)S(1)} %slice.272), channel_id=1, source_target_pairs={{0,16},{1,17},{2,18},{3,19},{4,20},{5,21},{6,22},{7,23},{8,24},{9,... | collective-permute-start | bytes 73736 | tf_op jit(solution)/shard_map/ppermute | solution.py:23
  31.1 11.1 %collective-permute-start.5 = (bf16[33,1,256]{2,1,0:T(2,128)(2,1)S(1)}, bf16[33,1,256]{2,1,0:T(2,128)(2,1)S(1)}, u32[]{:S(2)}, u32[]{:S(2)}) collective-permute-start(bf16[33,1,256]{2,1,0:T(2,128)(2,1)S(1)} %fusion.66), channel_id=1, source_target_pairs={{0,1},{1,2},{2,3},{3,4},{4,5},{5,6},{6,7},{7,8},{8,9},{9,10},{10,1... | collective-permute-start | bytes 50696 | tf_op jit(solution)/shard_map/ppermute | solution.py:23
  42.7 3.2 %copy-start.3 = (bf16[16,24,256]{2,1,0:T(8,128)(2,1)S(1)}, bf16[16,24,256]{2,1,0:T(8,128)(2,1)}, u32[]{:S(2)}) copy-start(bf16[16,24,256]{2,1,0:T(8,128)(2,1)} %slice.227) | copy-start | bytes 589828
  44.5 2.6 %copy-start.1 = (bf16[3,3,256,512]{3,2,1,0:T(8,128)(2,1)S(1)}, bf16[3,3,256,512]{3,2,1,0:T(8,128)(2,1)}, u32[]{:S(2)}) copy-start(bf16[3,3,256,512]{3,2,1,0:T(8,128)(2,1)} %param.10) | copy-start | bytes 7077892
  48.2 0.7 copy-start.5
  78.8 10.8 %collective-permute-start.6 = (bf16[1,384,32]{1,2,0:T(8,128)(2,1)S(1)}, bf16[1,384,32]{1,2,0:T(8,128)(2,1)S(1)}, u32[]{:S(2)}, u32[]{:S(2)}) collective-permute-start(bf16[1,384,32]{1,2,0:T(8,128)(2,1)S(1)} %slice.242), channel_id=1, source_target_pairs={{0,16},{1,17},{2,18},{3,19},{4,20},{5,21},{6,22},{7,23},{8,24},{9,... | collective-permute-start | bytes 73736 | tf_op jit(solution)/shard_map/ppermute | solution.py:12
  82.0 7.6 %collective-permute-start.7 = (bf16[1,384,32]{1,2,0:T(8,128)(2,1)S(1)}, bf16[1,384,32]{1,2,0:T(8,128)(2,1)S(1)}, u32[]{:S(2)}, u32[]{:S(2)}) collective-permute-start(bf16[1,384,32]{1,2,0:T(8,128)(2,1)S(1)} %slice.244), channel_id=1, source_target_pairs={{16,0},{17,1},{18,2},{19,3},{20,4},{21,5},{22,6},{23,7},{24,8},{25... | collective-permute-start | bytes 73736 | tf_op jit(solution)/shard_map/ppermute | solution.py:15
  86.2 3.8 %copy-start.4 = (bf16[1,3,3,32,32]{4,3,2,1,0:T(8,128)(2,1)S(1)}, bf16[1,3,3,32,32]{4,3,2,1,0:T(8,128)(2,1)}, u32[]{:S(2)}) copy-start(bf16[1,3,3,32,32]{4,3,2,1,0:T(8,128)(2,1)} %param.12) | copy-start | bytes 55300
  91.8 0.7 copy-start.7
where the time goes:
time: 94.2 us; the launch traced here: 93.5 us
  local copies, waits for them, and re-layouts  30.4 us (32%)
  starting transfers between devices  18.9 us (20%)
  blocking collectives  17.8 us (19%)
  matrix products  12.2 us (13%)
  waiting for transfers between devices  7.24 us (8%)
  other arithmetic  6.36 us (7%)
    all_to_all x1, blocking collectives, on_device(): lax.all_to_all(layer_two, 'col', split_axis=2, concat_axis=1, tiled=True)  17.8 us
    slice x9, local copies, waits for them, and re-layouts, conv_taps(): lax.slice(padded, (tap_row, tap_col, 0), (tap_row + stride * (out_rows -...  9.99 us
    all_to_all x3, local copies, waits for them, and re-layouts, on_device(): lax.all_to_all(layer_two, 'col', split_axis=2, concat_axis=1, tiled=True)  9.22 us
    ppermute x3, starting transfers between devices, padded_2(): lax.ppermute(lax.slice_in_dim(block, block.shape[dim] - width, None, axis...  8.97 us
    dot_general x18, matrix products, conv_taps(): jnp.dot(window.reshape(out_rows * out_cols, padded.shape[2]), weight[tap_...  8.73 us
    ppermute x3, waiting for transfers between devices, padded_2(): lax.ppermute(lax.slice_in_dim(block, 0, width, axis=dim), axis, backward)  7.03 us
    unnamed x19, local copies, waits for them, and re-layouts  6.77 us
    ppermute x2, starting transfers between devices, passed_along(): return lax.ppermute(block, axis, route)  5.91 us
  transfers between devices with their start and end apart: 8, of which 3 were waited for; matrix products, arithmetic and copies ran while one was open for 14% of the time, Pallas kernels for 0%

commit v1 on v0

v1 whole, which is shorter than its diff:
```python
import functools

import jax
import jax.numpy as jnp
from jax import lax
from jax.experimental import pallas as pl
from jax.experimental.pallas import tpu as pltpu
from jax.sharding import PartitionSpec as P

MESH = pl.DeviceIdType.MESH
F32 = jnp.float32
BF16 = jnp.bfloat16


def dot(a, b):
    return jnp.dot(a, b, preferred_element_type=F32)


def kernel(
    rows, cols,
    feat, w1_hbm, b1, w2_hbm, b2, w3, b3, out,
    w1, w2, x32, st_l, st_r, rc_l, rc_r, rc_u, rc_d, taps, a2, l2, send, main, top, bot, l32, band,
    w_sem, h_send, h_recv, m_send, m_recv, t_send, t_recv, b_send, b_recv,
):
    row = lax.axis_index("row")
    col = lax.axis_index("col")
    tr, tc, ch = feat.shape
    half = tc // 2
    has_up, has_down = row > 0, row < rows - 1
    has_left, has_right = col > 0, col < cols - 1

    load_one = pltpu.make_async_copy(w1_hbm, w1, w_sem.at[0])
    load_two = pltpu.make_async_copy(w2_hbm, w2, w_sem.at[1])
    load_one.start()
    load_two.start()

    barrier = pltpu.get_barrier_semaphore()

    def greet(device_row, first):
        def body(k, carry):
            pl.semaphore_signal(
                barrier, inc=1, device_id=(device_row, lax.rem(col + k, cols)), device_id_type=MESH
            )
            return carry

        lax.fori_loop(first, cols, body, 0)

    greet(row, 1)
    pl.when(has_up)(lambda: greet(row - 1, 0))
    pl.when(has_down)(lambda: greet(row + 1, 0))

    lanes_of = [slice(128 * h, 128 * h + 128) for h in range(ch // 128)]
    for h, part in enumerate(lanes_of):
        x32[h, 2 : tr + 2, 8 : tc + 8, :] = feat[:, :, part].astype(F32)
        st_r[:, :, part] = x32[h, 2 : tr + 2, tc + 6 : tc + 8, :].astype(BF16)
        st_l[:, :, part] = x32[h, 2 : tr + 2, 8:10, :].astype(BF16)
    zero = lambda ref, lo, hi: ref.__setitem__(
        slice(lo, hi), jnp.zeros((hi - lo,) + ref.shape[1:], ref.dtype)
    )
    copies = []
    plan = (
        (feat.at[tr - 2 : tr], rc_u, 1, 0, has_down, has_up, (rc_u, 0, 2)),
        (feat.at[0:1], rc_d, -1, 0, has_up, has_down, (rc_d, 0, 1)),
        (st_r, rc_l.at[2 : tr + 2], 0, 1, has_right, has_left, (rc_l, 2, tr + 2)),
        (st_l, rc_r.at[2 : tr + 2], 0, -1, has_left, has_right, (rc_r, 2, tr + 2)),
        (st_r.at[tr - 2 : tr], rc_l.at[0:2], 1, 1, has_down & has_right, has_up & has_left, (rc_l, 0, 2)),
        (st_r.at[0:1], rc_l.at[tr + 2 : tr + 3], -1, 1, has_up & has_right, has_down & has_left, (rc_l, tr + 2, tr + 3)),
        (st_l.at[tr - 2 : tr], rc_r.at[0:2], 1, -1, has_down & has_left, has_up & has_right, (rc_r, 0, 2)),
        (st_l.at[0:1], rc_r.at[tr + 2 : tr + 3], -1, -1, has_up & has_left, has_down & has_right, (rc_r, tr + 2, tr + 3)),
    )
    for index, (src, dst, dr, dc, sends, gets, hole) in enumerate(plan):
        copy = pltpu.make_async_remote_copy(
            src_ref=src, dst_ref=dst, send_sem=h_send.at[index], recv_sem=h_recv.at[index],
            device_id=(row + dr, col + dc), device_id_type=MESH,
        )
        copies.append(copy)
        pl.when(jnp.logical_not(gets))(functools.partial(zero, *hole))

    reach = cols * (1 + has_up.astype(jnp.int32) + has_down.astype(jnp.int32)) - 1
    pl.semaphore_wait(barrier, reach)
    for copy, item in zip(copies, plan):
        pl.when(item[4])(copy.start)

    width = w3.shape[3]
    quad = 4 * width
    band[...] = jnp.zeros_like(band)
    for b in range(3):
        for a in range(3):
            block = w3[0, a, b]
            for i in range(4):
                at = (i + 3 + a) * width
                band[b, at : at + width, i * width : (i + 1) * width] = block
    bias3 = jnp.concatenate([b3[...]] * 4, axis=1)
    l32[0:8, :] = jnp.zeros((8, l32.shape[1]), F32)
    full = cols * half
    l32[full + 8 : full + 16, :] = jnp.zeros((8, l32.shape[1]), F32)

    @pl.when(jnp.logical_not(has_up))
    def _():
        top[...] = jnp.zeros_like(top)

    @pl.when(jnp.logical_not(has_down))
    def _():
        bot[...] = jnp.zeros_like(bot)

    for copy, item in zip(copies, plan):
        pl.when(item[5])(copy.wait_recv)
    for h, part in enumerate(lanes_of):
        x32[h, 0:2, 8 : tc + 8, :] = rc_u[:, :, part].astype(F32)
        x32[h, tr + 2 : tr + 3, 8 : tc + 8, :] = rc_d[:, :, part].astype(F32)
        x32[h, 0 : tr + 3, 6:8, :] = rc_l[:, :, part].astype(F32)
        x32[h, 0 : tr + 3, tc + 8 : tc + 10, :] = rc_r[:, :, part].astype(F32)

    for j in range(4):
        for r in range(0, tr + 4, 12):
            for h in range(ch // 128):
                taps[r : r + 12, :, j * ch + 128 * h : j * ch + 128 * h + 128] = x32[
                    h, r : r + 12, pl.ds(j + 6, 32, stride=2), :
                ].astype(BF16)

    load_one.wait()
    bias1 = b1[...]
    left_edge = jnp.logical_not(has_left)
    for first, pairs in ((0, 8), (8, tr // 2 - 7)):
        m = pairs * 64
        for parity in range(2):
            acc = None
            for a in range(3):
                lhs = taps[2 * first + a : 2 * first + a + 2 * pairs, :, parity * ch : (parity + 3) * ch]
                part = dot(lhs.reshape(m, 3 * ch), w1[a].reshape(3 * ch, ch))
                acc = part if acc is None else acc + part
            acc = jnp.maximum(acc + bias1, 0.0)
            if parity == 0:
                spot = lax.broadcasted_iota(jnp.int32, acc.shape, 0)
                acc = jnp.where((lax.rem(spot, 32) == 0) & left_edge, 0.0, acc)
                moved = pltpu.roll(acc, m - 1, 0)
                a2[first : first + pairs, :, :, 2 * ch : 3 * ch] = moved.astype(BF16).reshape(pairs, 2, 32, ch)
            a2[first : first + pairs, :, :, parity * ch : (parity + 1) * ch] = acc.astype(BF16).reshape(
                pairs, 2, 32, ch
            )

    @pl.when(jnp.logical_not(has_up))
    def _():
        a2[0, 0] = jnp.zeros(a2.shape[2:], BF16)

    load_two.wait()
    out_ch = w2.shape[3]
    orow = tr // 2
    acc = None
    for a in range(3):
        lhs = a2[a // 2 : a // 2 + orow, a % 2].reshape(orow * 32, 3 * ch)
        part = dot(lhs, w2[a].reshape(3 * ch, out_ch))
        acc = part if acc is None else acc + part
    l2[...] = jnp.maximum(acc + b2[...], 0.0).reshape(orow, 32, out_ch)

    for q in range(orow // 4):
        for g in range(cols):
            piece = jnp.concatenate(
                [l2[4 * q + r, 0:half, g * width : (g + 1) * width] for r in range(4)], axis=1
            )
            send[g, :, q * quad : (q + 1) * quad] = piece.astype(BF16)

    span = orow * width

    def main_copy(k):
        d = lax.rem(col + k, cols)
        return pltpu.make_async_remote_copy(
            src_ref=send.at[d], dst_ref=main.at[col], send_sem=m_send.at[k], recv_sem=m_recv.at[col],
            device_id=(row, d), device_id_type=MESH,
        )

    def main_arrival(k):
        s = lax.rem(col + k, cols)
        return pltpu.make_async_remote_copy(
            src_ref=send.at[s], dst_ref=main.at[s], send_sem=m_send.at[k], recv_sem=m_recv.at[s],
            device_id=(row, s), device_id_type=MESH,
        )

    def edge_copy(k, dr):
        d = lax.rem(col + k, cols)
        lanes = pl.ds(span - quad, quad) if dr > 0 else pl.ds(0, quad)
        there, ss, rs = (top, t_send, t_recv) if dr > 0 else (bot, b_send, b_recv)
        return pltpu.make_async_remote_copy(
            src_ref=send.at[d, :, lanes], dst_ref=there.at[col], send_sem=ss.at[k], recv_sem=rs.at[col],
            device_id=(row + dr, d), device_id_type=MESH,
        )

    def edge_arrival(k, dr):
        s = lax.rem(col + k, cols)
        there, ss, rs = (top, t_send, t_recv) if dr > 0 else (bot, b_send, b_recv)
        return pltpu.make_async_remote_copy(
            src_ref=there.at[s], dst_ref=there.at[s], send_sem=ss.at[k], recv_sem=rs.at[s],
            device_id=(row - dr, s), device_id_type=MESH,
        )

    def each(first, act):
        def body(k, carry):
            act(k)
            return carry

        lax.fori_loop(first, cols, body, 0)

    each(1, lambda k: main_copy(k).start())
    pl.when(has_down)(lambda: each(0, lambda k: edge_copy(k, 1).start()))
    pl.when(has_up)(lambda: each(0, lambda k: edge_copy(k, -1).start()))
    main[col] = send[col]
    each(1, lambda k: main_arrival(k).wait_recv())
    pl.when(has_up)(lambda: each(0, lambda k: edge_arrival(k, 1).wait_recv()))
    pl.when(has_down)(lambda: each(0, lambda k: edge_arrival(k, -1).wait_recv()))

    for s in range(cols):
        at = 8 + half * s
        l32[at : at + half, 0:quad] = top[s].astype(F32)
        l32[at : at + half, quad : quad + span] = main[s].astype(F32)
        l32[at : at + half, quad + span : 2 * quad + span] = bot[s].astype(F32)

    shifted = [l32[7 + b : 7 + b + full, :].astype(BF16) for b in range(3)]
    for q in range(orow // 4):
        acc = None
        for b in range(3):
            part = dot(shifted[b][:, q * quad : (q + 3) * quad], band[b])
            acc = part if acc is None else acc + part
        out[4 * q : 4 * q + 4] = (acc + bias3).T.reshape(4, width, full).astype(BF16)

    for copy, item in zip(copies, plan):
        pl.when(item[4])(copy.wait_send)
    each(1, lambda k: main_copy(k).wait_send())
    pl.when(has_down)(lambda: each(0, lambda k: edge_copy(k, 1).wait_send()))
    pl.when(has_up)(lambda: each(0, lambda k: edge_copy(k, -1).wait_send()))


def on_device(rows, cols, features, conv_one, bias_one, conv_two, bias_two, conv_three, bias_three):
    tr, tc, ch = features.shape
    c2 = conv_two.shape[3]
    width = conv_three.shape[3]
    half, orow = tc // 2, tr // 2
    full, span, quad = cols * half, orow * width, 4 * width
    vmem = pl.BlockSpec(memory_space=pltpu.VMEM)
    hbm = pl.BlockSpec(memory_space=pl.ANY)
    dma = pltpu.SemaphoreType.DMA
    return pl.pallas_call(
        functools.partial(kernel, rows, cols),
        out_shape=jax.ShapeDtypeStruct((orow, width, full), BF16),
        in_specs=[vmem, hbm, vmem, hbm, vmem, vmem, vmem],
        out_specs=vmem,
        scratch_shapes=[
            pltpu.VMEM(conv_one.shape, BF16),
            pltpu.VMEM(conv_two.shape, BF16),
            pltpu.VMEM((ch // 128, tr + 4, tc + 24, 128), F32),
            pltpu.VMEM((tr, 2, ch), BF16),
            pltpu.VMEM((tr, 2, ch), BF16),
            pltpu.VMEM((tr + 3, 2, ch), BF16),
            pltpu.VMEM((tr + 3, 2, ch), BF16),
            pltpu.VMEM((2, tc, ch), BF16),
            pltpu.VMEM((1, tc, ch), BF16),
            pltpu.VMEM((tr + 4, 32, 4 * ch), BF16),
            pltpu.VMEM((orow + 1, 2, 32, 3 * ch), BF16),
            pltpu.VMEM((orow, 32, c2), F32),
            pltpu.VMEM((cols, half, span), BF16),
            pltpu.VMEM((cols, half, span), BF16),
            pltpu.VMEM((cols, half, quad), BF16),
            pltpu.VMEM((cols, half, quad), BF16),
            pltpu.VMEM((full + 16, span + 2 * quad), F32),
            pltpu.VMEM((3, 3 * quad, quad), BF16),
            dma((2,)), dma((8,)), dma((8,)),
            dma((cols,)), dma((cols,)), dma((cols,)), dma((cols,)), dma((cols,)), dma((cols,)),
        ],
        compiler_params=pltpu.CompilerParams(
            collective_id=0, has_side_effects=True, vmem_limit_bytes=60 * 1024 * 1024
        ),
    )(
        features, conv_one, bias_one.reshape(1, -1), conv_two, bias_two.reshape(1, -1),
        conv_three, bias_three.reshape(1, -1),
    )


def solution(mesh):
    in_specs = (
        P("row", "col", None),
        P(),
        P(),
        P(),
        P(),
        P("col", None, None, None, None),
        P("col"),
    )
    return jax.shard_map(
        functools.partial(on_device, mesh.shape["row"], mesh.shape["col"]),
        mesh=mesh, in_specs=in_specs, out_specs=P("row", "col", None), check_vma=False,
    )
```

time: 94.2 us -> 33.6 us (0.36)
  Pallas kernels: 0 us -> 31.7 us
  local copies, waits for them, and re-layouts: 30.4 us -> 1.78 us
  starting transfers between devices: 18.9 us -> 0 us
  blocking collectives: 17.8 us -> 0 us
  matrix products: 12.2 us -> 0 us
  waiting for transfers between devices: 7.24 us -> 0 us
  other arithmetic: 6.36 us -> 0 us
    pallas_call x0 -> x1, Pallas kernels: none -> 31.7 us  [on_device(): pl.pallas_call(functools.partial(kernel, rows, cols), out_shape=jax.Shape...]
    ppermute x8 -> x0, starting transfers between devices: 18.9 us -> none  [the longest x3 8.97 us: padded_2(): lax.ppermute(lax.slice_in_dim(block, block.shape[dim] - width, None, axis...]
    all_to_all x1 -> x0, blocking collectives: 17.8 us -> none  [on_device(): lax.all_to_all(layer_two, 'col', split_axis=2, concat_axis=1, tiled=True)]
    slice x17 -> x0, local copies, waits for them, and re-layouts: 12.5 us -> none  [the longest x9 9.99 us: conv_taps(): lax.slice(padded, (tap_row, tap_col, 0), (tap_row + stride * (out_rows -...]
    dot_general x27 -> x0, matrix products: 12.2 us -> none  [the longest x18 8.73 us: conv_taps(): jnp.dot(window.reshape(out_rows * out_cols, padded.shape[2]), weight[tap_...]
    all_to_all x3 -> x0, local copies, waits for them, and re-layouts: 9.22 us -> none  [on_device(): lax.all_to_all(layer_two, 'col', split_axis=2, concat_axis=1, tiled=True)]
    ppermute x8 -> x0, waiting for transfers between devices: 7.24 us -> none  [the longest x3 7.03 us: padded_2(): lax.ppermute(lax.slice_in_dim(block, 0, width, axis=dim), axis, backward)]
    concatenate x6 -> x0, other arithmetic: 6.09 us -> none  [the longest x3 5.43 us: padded_2(): block = jnp.concatenate([low, block, high], axis=dim)]
  transfers between devices with their start and end apart: 8 -> 0, of which waited for: 3 -> 0; matrix products, arithmetic and copies ran while one was open for 14% -> 0% of each run, Pallas kernels for 0% -> 0%
where the time goes in v1:
time: 33.6 us; the launch traced here: 33.4 us
  Pallas kernels  31.7 us (94%)
  local copies, waits for them, and re-layouts  1.78 us (5%)
    pallas_call x1, Pallas kernels, on_device(): pl.pallas_call(functools.partial(kernel, rows, cols), out_shape=jax.Shape...  31.7 us
    unnamed x1, local copies, waits for them, and re-layouts  1.78 us

profile of v1, /device:TPU:0, one launch (start us, length us, event | category | flops | bytes accessed | tf_op | source)
XLA Modules:
  0.0 33.4 jit_solution(11233772572854688844)
XLA Ops:
  0.0 31.7 %shard_map.73 = bf16[16,32,384]{2,1,0:T(8,128)(2,1)} custom-call(bf16[32,48,256]{2,1,0:T(8,128)(2,1)} %feat.1, bf16[3,3,256,256]{3,2,1,0:T(8,128)(2,1)} %w1_hbm.1, f32[1,256]{1,0:T(1,128)} %bitcast.4, bf16[3,3,256,512]{3,2,1,0:T(8,128)(2,1)} %w2_hbm.1, f32[1,512]{1,0:T(1,128)} %bitcast.3, bf16[1,3,3,32,32]{4,3,2,1,0:T(8,128)(2,1)} %w3.1, f32[1,32]{1,0:T(1,128)} %bitcast.5), custom_call_target="tpu_custom_call" | custom-call | tf_op jit(solution)/shard_map/pallas_call | solution.py:241
  31.7 1.8 %copy.9 = bf16[16,32,384]{2,1,0:T(8,128)(2,1)} copy(bf16[16,32,384]{2,1,0:T(8,128)(2,1)} %shard_map.73) | data formatting | bytes 786432

commit v2 on v1

--- a/solution.py
+++ b/solution.py
@@ -19,7 +19,7 @@
 def kernel(
     rows, cols,
     feat, w1_hbm, b1, w2_hbm, b2, w3, b3, out,
-    w1, w2, x32, st_l, st_r, rc_l, rc_r, rc_u, rc_d, taps, a2, l2, send, main, top, bot, l32, band,
+    w1, w2, x32, st_l, st_r, rc_l, rc_r, rc_u, rc_d, taps, a2, l2, send, low, high, main, top, bot, l32, band,
     w_sem, h_send, h_recv, m_send, m_recv, t_send, t_recv, b_send, b_recv,
 ):
     row = lax.axis_index("row")
@@ -121,7 +121,12 @@
     load_one.wait()
     bias1 = b1[...]
     left_edge = jnp.logical_not(has_left)
-    for first, pairs in ((0, 8), (8, tr // 2 - 7)):
+    out_ch = w2.shape[3]
+    orow = tr // 2
+    span = orow * width
+    third = half // 3
+
+    def first_layer(first, pairs):
         m = pairs * 64
         for parity in range(2):
             acc = None
@@ -139,57 +144,60 @@
                 pairs, 2, 32, ch
             )
 
-    @pl.when(jnp.logical_not(has_up))
-    def _():
-        a2[0, 0] = jnp.zeros(a2.shape[2:], BF16)
-
-    load_two.wait()
-    out_ch = w2.shape[3]
-    orow = tr // 2
-    acc = None
-    for a in range(3):
-        lhs = a2[a // 2 : a // 2 + orow, a % 2].reshape(orow * 32, 3 * ch)
-        part = dot(lhs, w2[a].reshape(3 * ch, out_ch))
-        acc = part if acc is None else acc + part
-    l2[...] = jnp.maximum(acc + b2[...], 0.0).reshape(orow, 32, out_ch)
-
-    for q in range(orow // 4):
+    def second_layer(first, count):
+        acc = None
+        for a in range(3):
+            lhs = a2[first + a // 2 : first + a // 2 + count, a % 2].reshape(count * 32, 3 * ch)
+            part = dot(lhs, w2[a].reshape(3 * ch, out_ch))
+            acc = part if acc is None else acc + part
+        l2[first : first + count] = jnp.maximum(acc + b2[...], 0.0).reshape(count, 32, out_ch)
+
+    def pack(p):
+        for q in range(orow // 8):
+            for g in range(cols):
+                piece = jnp.concatenate(
+                    [
+                        l2[p * orow // 2 + 4 * q + r, 0:half, g * width : (g + 1) * width]
+                        for r in range(4)
+                    ],
+                    axis=1,
+                )
+                send[p, g, :, q * quad : (q + 1) * quad] = piece.astype(BF16)
+
+    def pack_edge(there, r):
         for g in range(cols):
-            piece = jnp.concatenate(
-                [l2[4 * q + r, 0:half, g * width : (g + 1) * width] for r in range(4)], axis=1
-            )
-            send[g, :, q * quad : (q + 1) * quad] = piece.astype(BF16)
-
-    span = orow * width
-
-    def main_copy(k):
+            pieces = [
+                l2[r, third * t : third * (t + 1), g * width : (g + 1) * width] for t in (0, 1, 2, 2)
+            ]
+            there[g] = jnp.concatenate(pieces, axis=1).astype(BF16)
+
+    def main_copy(p, k):
         d = lax.rem(col + k, cols)
         return pltpu.make_async_remote_copy(
-            src_ref=send.at[d], dst_ref=main.at[col], send_sem=m_send.at[k], recv_sem=m_recv.at[col],
-            device_id=(row, d), device_id_type=MESH,
-        )
-
-    def main_arrival(k):
+            src_ref=send.at[p, d], dst_ref=main.at[p, col], send_sem=m_send.at[p, k],
+            recv_sem=m_recv.at[p, col], device_id=(row, d), device_id_type=MESH,
+        )
+
+    def main_arrival(p, k):
         s = lax.rem(col + k, cols)
         return pltpu.make_async_remote_copy(
-            src_ref=send.at[s], dst_ref=main.at[s], send_sem=m_send.at[k], recv_sem=m_recv.at[s],
-            device_id=(row, s), device_id_type=MESH,
+            src_ref=send.at[p, s], dst_ref=main.at[p, s], send_sem=m_send.at[p, k],
+            recv_sem=m_recv.at[p, s], device_id=(row, s), device_id_type=MESH,
         )
 
     def edge_copy(k, dr):
         d = lax.rem(col + k, cols)
-        lanes = pl.ds(span - quad, quad) if dr > 0 else pl.ds(0, quad)
-        there, ss, rs = (top, t_send, t_recv) if dr > 0 else (bot, b_send, b_recv)
+        src, there, ss, rs = (high, top, t_send, t_recv) if dr > 0 else (low, bot, b_send, b_recv)
         return pltpu.make_async_remote_copy(
-            src_ref=send.at[d, :, lanes], dst_ref=there.at[col], send_sem=ss.at[k], recv_sem=rs.at[col],
+            src_ref=src.at[d], dst_ref=there.at[col], send_sem=ss.at[k], recv_sem=rs.at[col],
             device_id=(row + dr, d), device_id_type=MESH,
         )
 
     def edge_arrival(k, dr):
         s = lax.rem(col + k, cols)
-        there, ss, rs = (top, t_send, t_recv) if dr > 0 else (bot, b_send, b_recv)
+        src, there, ss, rs = (high, top, t_send, t_recv) if dr > 0 else (low, bot, b_send, b_recv)
         return pltpu.make_async_remote_copy(
-            src_ref=there.at[s], dst_ref=there.at[s], send_sem=ss.at[k], recv_sem=rs.at[s],
+            src_ref=src.at[s], dst_ref=there.at[s], send_sem=ss.at[k], recv_sem=rs.at[s],
             device_id=(row - dr, s), device_id_type=MESH,
         )
 
@@ -200,19 +208,47 @@
 
         lax.fori_loop(first, cols, body, 0)
 
-    each(1, lambda k: main_copy(k).start())
+    def clear_top():
+        a2[0, 0] = jnp.zeros(a2.shape[2:], BF16)
+
+    cut = orow // 2 + 1
+    first_layer(0, cut)
+    pl.when(jnp.logical_not(has_up))(clear_top)
+    load_two.wait()
+    second_layer(0, orow // 2)
+    pack(0)
+    each(1, lambda k: main_copy(0, k).start())
+    pack_edge(low, 0)
+    pl.when(has_up)(lambda: each(0, lambda k: edge_copy(k, -1).start()))
+    first_layer(cut, orow + 1 - cut)
+    second_layer(orow // 2, orow // 2)
+    pack(1)
+    each(1, lambda k: main_copy(1, k).start())
+    pack_edge(high, orow - 1)
     pl.when(has_down)(lambda: each(0, lambda k: edge_copy(k, 1).start()))
-    pl.when(has_up)(lambda: each(0, lambda k: edge_copy(k, -1).start()))
-    main[col] = send[col]
-    each(1, lambda k: main_arrival(k).wait_recv())
-    pl.when(has_up)(lambda: each(0, lambda k: edge_arrival(k, 1).wait_recv()))
-    pl.when(has_down)(lambda: each(0, lambda k: edge_arrival(k, -1).wait_recv()))
-
+    main[0, col] = send[0, col]
+    main[1, col] = send[1, col]
+
+    end = quad + span
+    l32[:, 0 : quad] = jnp.zeros((l32.shape[0], quad), F32)
+    l32[:, end : end + quad] = jnp.zeros((l32.shape[0], quad), F32)
+    each(1, lambda k: main_arrival(0, k).wait_recv())
     for s in range(cols):
         at = 8 + half * s
-        l32[at : at + half, 0:quad] = top[s].astype(F32)
-        l32[at : at + half, quad : quad + span] = main[s].astype(F32)
-        l32[at : at + half, quad + span : 2 * quad + span] = bot[s].astype(F32)
+        l32[at : at + half, quad : quad + span // 2] = main[0, s].astype(F32)
+    pl.when(has_down)(lambda: each(0, lambda k: edge_arrival(k, -1).wait_recv()))
+    for s in range(cols):
+        for t in range(3):
+            at = 8 + half * s + third * t
+            l32[at : at + third, end : end + width] = bot[s, :, t * width : (t + 1) * width].astype(F32)
+    each(1, lambda k: main_arrival(1, k).wait_recv())
+    pl.when(has_up)(lambda: each(0, lambda k: edge_arrival(k, 1).wait_recv()))
+    for s in range(cols):
+        at = 8 + half * s
+        l32[at : at + half, quad + span // 2 : end] = main[1, s].astype(F32)
+        for t in range(3):
+            at = 8 + half * s + third * t
+            l32[at : at + third, quad - width : quad] = top[s, :, t * width : (t + 1) * width].astype(F32)
 
     shifted = [l32[7 + b : 7 + b + full, :].astype(BF16) for b in range(3)]
     for q in range(orow // 4):
@@ -224,7 +260,8 @@
 
     for copy, item in zip(copies, plan):
         pl.when(item[4])(copy.wait_send)
-    each(1, lambda k: main_copy(k).wait_send())
+    each(1, lambda k: main_copy(0, k).wait_send())
+    each(1, lambda k: main_copy(1, k).wait_send())
     pl.when(has_down)(lambda: each(0, lambda k: edge_copy(k, 1).wait_send()))
     pl.when(has_up)(lambda: each(0, lambda k: edge_copy(k, -1).wait_send()))
 
@@ -256,14 +293,16 @@
             pltpu.VMEM((tr + 4, 32, 4 * ch), BF16),
             pltpu.VMEM((orow + 1, 2, 32, 3 * ch), BF16),
             pltpu.VMEM((orow, 32, c2), F32),
-            pltpu.VMEM((cols, half, span), BF16),
-            pltpu.VMEM((cols, half, span), BF16),
-            pltpu.VMEM((cols, half, quad), BF16),
-            pltpu.VMEM((cols, half, quad), BF16),
+            pltpu.VMEM((2, cols, half, span // 2), BF16),
+            pltpu.VMEM((cols, half // 3, quad), BF16),
+            pltpu.VMEM((cols, half // 3, quad), BF16),
+            pltpu.VMEM((2, cols, half, span // 2), BF16),
+            pltpu.VMEM((cols, half // 3, quad), BF16),
+            pltpu.VMEM((cols, half // 3, quad), BF16),
             pltpu.VMEM((full + 16, span + 2 * quad), F32),
             pltpu.VMEM((3, 3 * quad, quad), BF16),
             dma((2,)), dma((8,)), dma((8,)),
-            dma((cols,)), dma((cols,)), dma((cols,)), dma((cols,)), dma((cols,)), dma((cols,)),
+            dma((2, cols)), dma((2, cols)), dma((cols,)), dma((cols,)), dma((cols,)), dma((cols,)),
         ],
         compiler_params=pltpu.CompilerParams(
             collective_id=0, has_side_effects=True, vmem_limit_bytes=60 * 1024 * 1024

time: 33.6 us -> 29.4 us (0.87)
  Pallas kernels: 31.7 us -> 27.4 us
    pallas_call x1, Pallas kernels: 31.7 us -> 27.4 us  [on_device(): pl.pallas_call(functools.partial(kernel, rows, cols), out_shape=jax.Shape...]
where the time goes in v2:
time: 29.4 us; the launch traced here: 29.2 us
  Pallas kernels  27.4 us (93%)
  local copies, waits for them, and re-layouts  1.78 us (6%)
    pallas_call x1, Pallas kernels, on_device(): pl.pallas_call(functools.partial(kernel, rows, cols), out_shape=jax.Shape...  27.4 us
    unnamed x1, local copies, waits for them, and re-layouts  1.78 us

profile of v2, /device:TPU:0, one launch (start us, length us, event | category | flops | bytes accessed | tf_op | source)
XLA Modules:
  0.0 29.2 jit_solution(10278946483657199769)
XLA Ops:
  0.0 27.4 %shard_map.73 = bf16[16,32,384]{2,1,0:T(8,128)(2,1)} custom-call(bf16[32,48,256]{2,1,0:T(8,128)(2,1)} %feat.1, bf16[3,3,256,256]{3,2,1,0:T(8,128)(2,1)} %w1_hbm.1, f32[1,256]{1,0:T(1,128)} %bitcast.4, bf16[3,3,256,512]{3,2,1,0:T(8,128)(2,1)} %w2_hbm.1, f32[1,512]{1,0:T(1,128)} %bitcast.3, bf16[1,3,3,32,32]{4,3,2,1,0:T(8,128)(2,1)} %w3.1, f32[1,32]{1,0:T(1,128)} %bitcast.5), custom_call_target="tpu_custom_call" | custom-call | tf_op jit(solution)/shard_map/pallas_call | solution.py:278
  27.4 1.8 %copy.9 = bf16[16,32,384]{2,1,0:T(8,128)(2,1)} copy(bf16[16,32,384]{2,1,0:T(8,128)(2,1)} %shard_map.73) | data formatting | bytes 786432

commit v3 on v2

--- a/solution.py
+++ b/solution.py
@@ -18,8 +18,8 @@
 
 def kernel(
     rows, cols,
-    feat, w1_hbm, b1, w2_hbm, b2, w3, b3, out,
-    w1, w2, x32, st_l, st_r, rc_l, rc_r, rc_u, rc_d, taps, a2, l2, send, low, high, main, top, bot, l32, band,
+    feat_hbm, w1_hbm, b1_hbm, w2_hbm, b2_hbm, w3_hbm, b3_hbm, out,
+    feat, w1, b1, w2, b2, w3, b3, x32, st_l, st_r, rc_l, rc_r, rc_u, rc_d, taps, a2, l2, send, low, high, main, top, bot, l32, band,
     w_sem, h_send, h_recv, m_send, m_recv, t_send, t_recv, b_send, b_recv,
 ):
     row = lax.axis_index("row")
@@ -29,10 +29,16 @@
     has_up, has_down = row > 0, row < rows - 1
     has_left, has_right = col > 0, col < cols - 1
 
-    load_one = pltpu.make_async_copy(w1_hbm, w1, w_sem.at[0])
-    load_two = pltpu.make_async_copy(w2_hbm, w2, w_sem.at[1])
-    load_one.start()
-    load_two.start()
+    load_feat, load_w3, load_b3, load_b1, load_one, load_b2, load_two = [
+        pltpu.make_async_copy(src, dst, w_sem.at[index])
+        for index, (src, dst) in enumerate(
+            (
+                (feat_hbm, feat), (w3_hbm, w3), (b3_hbm, b3), (b1_hbm, b1),
+                (w1_hbm, w1), (b2_hbm, b2), (w2_hbm, w2),
+            )
+        )
+    ]
+    load_feat.start()
 
     barrier = pltpu.get_barrier_semaphore()
 
@@ -48,6 +54,9 @@
     greet(row, 1)
     pl.when(has_up)(lambda: greet(row - 1, 0))
     pl.when(has_down)(lambda: greet(row + 1, 0))
+    for load in (load_w3, load_b3, load_b1, load_one, load_b2, load_two):
+        load.start()
+    load_feat.wait()
 
     lanes_of = [slice(128 * h, 128 * h + 128) for h in range(ch // 128)]
     for h, part in enumerate(lanes_of):
@@ -81,6 +90,8 @@
     for copy, item in zip(copies, plan):
         pl.when(item[4])(copy.start)
 
+    load_w3.wait()
+    load_b3.wait()
     width = w3.shape[3]
     quad = 4 * width
     band[...] = jnp.zeros_like(band)
@@ -118,6 +129,7 @@
                     h, r : r + 12, pl.ds(j + 6, 32, stride=2), :
                 ].astype(BF16)
 
+    load_b1.wait()
     load_one.wait()
     bias1 = b1[...]
     left_edge = jnp.logical_not(has_left)
@@ -153,16 +165,11 @@
         l2[first : first + count] = jnp.maximum(acc + b2[...], 0.0).reshape(count, 32, out_ch)
 
     def pack(p):
-        for q in range(orow // 8):
-            for g in range(cols):
-                piece = jnp.concatenate(
-                    [
-                        l2[p * orow // 2 + 4 * q + r, 0:half, g * width : (g + 1) * width]
-                        for r in range(4)
-                    ],
-                    axis=1,
-                )
-                send[p, g, :, q * quad : (q + 1) * quad] = piece.astype(BF16)
+        for g in range(cols):
+            piece = jnp.concatenate(
+                [l2[4 * p + r, 0:half, g * width : (g + 1) * width] for r in range(4)], axis=1
+            )
+            send[p, g] = piece.astype(BF16)
 
     def pack_edge(there, r):
         for g in range(cols):
@@ -171,17 +178,16 @@
             ]
             there[g] = jnp.concatenate(pieces, axis=1).astype(BF16)
 
-    def main_copy(p, k):
-        d = lax.rem(col + k, cols)
+    def main_copy(p, d):
         return pltpu.make_async_remote_copy(
-            src_ref=send.at[p, d], dst_ref=main.at[p, col], send_sem=m_send.at[p, k],
+            src_ref=send.at[p, d], dst_ref=main.at[p, col], send_sem=m_send.at[p, d],
             recv_sem=m_recv.at[p, col], device_id=(row, d), device_id_type=MESH,
         )
 
     def main_arrival(p, k):
         s = lax.rem(col + k, cols)
         return pltpu.make_async_remote_copy(
-            src_ref=send.at[p, s], dst_ref=main.at[p, s], send_sem=m_send.at[p, k],
+            src_ref=send.at[p, s], dst_ref=main.at[p, s], send_sem=m_send.at[p, s],
             recv_sem=m_recv.at[p, s], device_id=(row, s), device_id_type=MESH,
         )
 
@@ -211,41 +217,58 @@
     def clear_top():
         a2[0, 0] = jnp.zeros(a2.shape[2:], BF16)
 
-    cut = orow // 2 + 1
-    first_layer(0, cut)
-    pl.when(jnp.logical_not(has_up))(clear_top)
-    load_two.wait()
-    second_layer(0, orow // 2)
-    pack(0)
-    each(1, lambda k: main_copy(0, k).start())
-    pack_edge(low, 0)
-    pl.when(has_up)(lambda: each(0, lambda k: edge_copy(k, -1).start()))
-    first_layer(cut, orow + 1 - cut)
-    second_layer(orow // 2, orow // 2)
-    pack(1)
-    each(1, lambda k: main_copy(1, k).start())
-    pack_edge(high, orow - 1)
-    pl.when(has_down)(lambda: each(0, lambda k: edge_copy(k, 1).start()))
-    main[0, col] = send[0, col]
-    main[1, col] = send[1, col]
+    part = cols // 2
+    own = col // part
+
+    def send_far(p):
+        def body(k, carry):
+            main_copy(p, (1 - own) * part + lax.rem(col + k, part)).start()
+            return carry
+
+        lax.fori_loop(0, part, body, 0)
+
+    def send_near(p):
+        def body(k, carry):
+            main_copy(p, own * part + lax.rem(col + k, part)).start()
+            return carry
+
+        lax.fori_loop(1, part, body, 0)
+
+    chunks = orow // 4
+    for p in range(chunks):
+        first_layer(4 * p + (p > 0), 4 + (p == 0))
+        if p == 0:
+            pl.when(jnp.logical_not(has_up))(clear_top)
+            load_b2.wait()
+            load_two.wait()
+        second_layer(4 * p, 4)
+        pack(p)
+        send_far(p)
+        send_near(p)
+        if p == 0:
+            pack_edge(low, 0)
+            pl.when(has_up)(lambda: each(0, lambda k: edge_copy(k, -1).start()))
+        if p == chunks - 1:
+            pack_edge(high, orow - 1)
+            pl.when(has_down)(lambda: each(0, lambda k: edge_copy(k, 1).start()))
+        main[p, col] = send[p, col]
 
     end = quad + span
-    l32[:, 0 : quad] = jnp.zeros((l32.shape[0], quad), F32)
+    l32[:, 0:quad] = jnp.zeros((l32.shape[0], quad), F32)
     l32[:, end : end + quad] = jnp.zeros((l32.shape[0], quad), F32)
-    each(1, lambda k: main_arrival(0, k).wait_recv())
-    for s in range(cols):
-        at = 8 + half * s
-        l32[at : at + half, quad : quad + span // 2] = main[0, s].astype(F32)
-    pl.when(has_down)(lambda: each(0, lambda k: edge_arrival(k, -1).wait_recv()))
-    for s in range(cols):
-        for t in range(3):
-            at = 8 + half * s + third * t
-            l32[at : at + third, end : end + width] = bot[s, :, t * width : (t + 1) * width].astype(F32)
-    each(1, lambda k: main_arrival(1, k).wait_recv())
+    for p in range(chunks):
+        each(1, lambda k: main_arrival(p, k).wait_recv())
+        for s in range(cols):
+            at = 8 + half * s
+            l32[at : at + half, quad * (p + 1) : quad * (p + 2)] = main[p, s].astype(F32)
+        if p == 0:
+            pl.when(has_down)(lambda: each(0, lambda k: edge_arrival(k, -1).wait_recv()))
+            for s in range(cols):
+                for t in range(3):
+                    at = 8 + half * s + third * t
+                    l32[at : at + third, end : end + width] = bot[s, :, t * width : (t + 1) * width].astype(F32)
     pl.when(has_up)(lambda: each(0, lambda k: edge_arrival(k, 1).wait_recv()))
     for s in range(cols):
-        at = 8 + half * s
-        l32[at : at + half, quad + span // 2 : end] = main[1, s].astype(F32)
         for t in range(3):
             at = 8 + half * s + third * t
             l32[at : at + third, quad - width : quad] = top[s, :, t * width : (t + 1) * width].astype(F32)
@@ -260,8 +283,8 @@
 
     for copy, item in zip(copies, plan):
         pl.when(item[4])(copy.wait_send)
-    each(1, lambda k: main_copy(0, k).wait_send())
-    each(1, lambda k: main_copy(1, k).wait_send())
+    for p in range(chunks):
+        each(1, lambda k: main_copy(p, lax.rem(col + k, cols)).wait_send())
     pl.when(has_down)(lambda: each(0, lambda k: edge_copy(k, 1).wait_send()))
     pl.when(has_up)(lambda: each(0, lambda k: edge_copy(k, -1).wait_send()))
 
@@ -278,11 +301,16 @@
     return pl.pallas_call(
         functools.partial(kernel, rows, cols),
         out_shape=jax.ShapeDtypeStruct((orow, width, full), BF16),
-        in_specs=[vmem, hbm, vmem, hbm, vmem, vmem, vmem],
+        in_specs=[hbm] * 7,
         out_specs=vmem,
         scratch_shapes=[
+            pltpu.VMEM(features.shape, BF16),
             pltpu.VMEM(conv_one.shape, BF16),
+            pltpu.VMEM((1, ch), F32),
             pltpu.VMEM(conv_two.shape, BF16),
+            pltpu.VMEM((1, c2), F32),
+            pltpu.VMEM(conv_three.shape, BF16),
+            pltpu.VMEM((1, width), F32),
             pltpu.VMEM((ch // 128, tr + 4, tc + 24, 128), F32),
             pltpu.VMEM((tr, 2, ch), BF16),
             pltpu.VMEM((tr, 2, ch), BF16),
@@ -293,16 +321,16 @@
             pltpu.VMEM((tr + 4, 32, 4 * ch), BF16),
             pltpu.VMEM((orow + 1, 2, 32, 3 * ch), BF16),
             pltpu.VMEM((orow, 32, c2), F32),
-            pltpu.VMEM((2, cols, half, span // 2), BF16),
+            pltpu.VMEM((orow // 4, cols, half, quad), BF16),
             pltpu.VMEM((cols, half // 3, quad), BF16),
             pltpu.VMEM((cols, half // 3, quad), BF16),
-            pltpu.VMEM((2, cols, half, span // 2), BF16),
+            pltpu.VMEM((orow // 4, cols, half, quad), BF16),
             pltpu.VMEM((cols, half // 3, quad), BF16),
             pltpu.VMEM((cols, half // 3, quad), BF16),
             pltpu.VMEM((full + 16, span + 2 * quad), F32),
             pltpu.VMEM((3, 3 * quad, quad), BF16),
-            dma((2,)), dma((8,)), dma((8,)),
-            dma((2, cols)), dma((2, cols)), dma((cols,)), dma((cols,)), dma((cols,)), dma((cols,)),
+            dma((7,)), dma((8,)), dma((8,)),
+            dma((orow // 4, cols)), dma((orow // 4, cols)), dma((cols,)), dma((cols,)), dma((cols,)), dma((cols,)),
         ],
         compiler_params=pltpu.CompilerParams(
             collective_id=0, has_side_effects=True, vmem_limit_bytes=60 * 1024 * 1024

time: 29.4 us -> 29.2 us (level)
  no operation moved by 1% of the time
where the time goes in v3:
time: 29.2 us; the launch traced here: 29 us
  Pallas kernels  27.2 us (93%)
  local copies, waits for them, and re-layouts  1.78 us (6%)
    pallas_call x1, Pallas kernels, on_device(): pl.pallas_call(functools.partial(kernel, rows, cols), out_shape=jax.Shape...  27.2 us
    unnamed x1, local copies, waits for them, and re-layouts  1.78 us

profile of v3, /device:TPU:0, one launch (start us, length us, event | category | flops | bytes accessed | tf_op | source)
XLA Modules:
  0.0 29.0 jit_solution(1877134622160624080)
XLA Ops:
  0.0 27.2 %shard_map.73 = bf16[16,32,384]{2,1,0:T(8,128)(2,1)} custom-call(bf16[32,48,256]{2,1,0:T(8,128)(2,1)} %feat_hbm.1, bf16[3,3,256,256]{3,2,1,0:T(8,128)(2,1)} %w1_hbm.1, f32[1,256]{1,0:T(1,128)} %bitcast.4, bf16[3,3,256,512]{3,2,1,0:T(8,128)(2,1)} %w2_hbm.1, f32[1,512]{1,0:T(1,128)} %bitcast.3, bf16[1,3,3,32,32]{4,3,2,1,0:T(8,128)(2,1)} %w3_hbm.1, f32[1,32]{1,0:T(1,128)} %bitcast.5), custom_call_target="tpu_custom_call" | custom-call | tf_op jit(solution)/shard_map/pallas_call | solution.py:301
  27.2 1.8 %copy.9 = bf16[16,32,384]{2,1,0:T(8,128)(2,1)} copy(bf16[16,32,384]{2,1,0:T(8,128)(2,1)} %shard_map.73) | data formatting | bytes 786432
